TPU v7x, 32 devices: a whole 2x2x4 slice. The times are simulated.
32 devices in a mesh: frame: 8 (over z, core), tok: 4 (over y, x).
Axes of the slice: x: 2, y: 2, z: 4, core: 2. Of those that a mesh axis runs over, the one named last changes fastest.
Arguments:
- stream: bfloat16 [8, 1024, 1152], P('frame', 'tok'), may hold values from -20 to 20
- queries: bfloat16 [8, 1024, 1152], P('frame', 'tok'), may hold values from -200 to 200
- key_vectors: bfloat16 [8, 1024, 1152], P('frame', 'tok'), may hold values from -6 to 6
- value_vectors: bfloat16 [8, 1024, 1152], P('frame', 'tok'), may hold values from -6 to 6
- modulation: float32 [8, 4, 1152], P('frame'), may hold values from -4 to 4
- output_weight: bfloat16 [1152, 1152], replicated, may hold values from -0.1875 to 0.1875
- output_bias: float32 [1152], replicated, may hold values from -3 to 3
- router_weight: bfloat16 [1152, 8], replicated, may hold values from -0.1875 to 0.1875
- expand_weight: bfloat16 [8, 1152, 4608], P('frame', None, 'tok'), may hold values from -0.1875 to 0.1875
- expand_bias: float32 [8, 4608], P('frame', 'tok'), may hold values from -3 to 3
- reduce_weight: bfloat16 [8, 4608, 1152], P('frame', 'tok'), may hold values from -0.09375 to 0.09375
- reduce_bias: float32 [8, 1152], P('frame'), may hold values from -3 to 3
- counts: int32 [8, 8], P(None, 'frame'), may hold values from 1 to 96, 256 in all within a row
- picked_rows: int32 [8, 8, 96], P(None, 'frame'), may hold values from 0 to 1023, as said below
Outputs:
- layer_out: bfloat16 [8, 1024, 1152], P('frame', 'tok')
Inputs may be any that keep to these rules, and one draw needn't show every extreme that they name: counts[e, g] slots of block (e, g) are used; the counts of one expert sum to 256. The entries of one block picked_rows[e, g, :] are distinct positions among the 1024 tokens of frame g; slots at or beyond counts[e, g] are unused.
All inputs are finite; a program needn't handle non-finite values.
Results may differ from a plain program's by a relative error of at most 0.0055.
Values may be sent and summed in bfloat16 or wider, within the bound.
A program may use at most 64 MiB of HBM per device.

v0:
```python
import math

import jax
import jax.numpy as jnp
from jax import lax
from jax.experimental import pallas as pl
from jax.experimental.pallas import tpu as pltpu
from jax.sharding import PartitionSpec as P

H = 16
HD = 72
CAP = 256
BF = jnp.bfloat16
F32 = jnp.float32


def dot(a, b, ca, cb):
    return lax.dot_general(a, b, (((ca,), (cb,)), ((), ())), preferred_element_type=F32)


MESH = pl.DeviceIdType.MESH


def gelu(x):
    return 0.5 * x * (1.0 + jnp.tanh(math.sqrt(2.0 / math.pi) * (x + 0.044715 * (x * x * x))))


def packed_shape(slots, cols):
    full, rest = cols // 128, cols % 128
    if full and rest and 128 % rest == 0 and slots % (128 // rest) == 0:
        if slots * rest // 128 % 8 == 0 and slots % 16 == 0:
            return (full * slots + slots * rest // 128, 128)
    return (slots, cols)


def put_block(ref, at, x, slots):
    cols = x.shape[1]
    if ref.shape[1:] == (slots, cols):
        ref[at] = x.astype(BF)
        return
    full, rest = cols // 128, cols % 128
    for i in range(full):
        ref[at, i * slots : (i + 1) * slots, :] = x[:, i * 128 : (i + 1) * 128].astype(BF)
    high = slots * rest // 128
    tail = [x[i * high : (i + 1) * high, full * 128 :] for i in range(128 // rest)]
    ref[at, full * slots : full * slots + high, :] = jnp.concatenate(tail, axis=1).astype(BF)


def get_block(ref, at, slots, cols):
    if ref.shape[1:] == (slots, cols):
        return ref[at]
    full, rest = cols // 128, cols % 128
    high = slots * rest // 128
    parts = [ref[at, i * slots : (i + 1) * slots, :] for i in range(full)]
    tail = ref[at, full * slots : full * slots + high, :].astype(F32)
    tail = [tail[:, i * rest : (i + 1) * rest] for i in range(128 // rest)]
    return jnp.concatenate(parts + [jnp.concatenate(tail, axis=0).astype(BF)], axis=1)


def layer_kernel(
    q_ref,
    k_ref,
    v_ref,
    stream_ref,
    mod_ref,
    out_bias_ref,
    router_ref,
    expand_bias_ref,
    reduce_bias_row,
    own_counts_ref,
    picked_ref,
    wo_hbm,
    we_hbm,
    wr_hbm,
    o_ref,
    wo,
    we,
    wr,
    qkv_out,
    qkv_in,
    att_out,
    att_in,
    picks,
    packs,
    packs_turned,
    normed_out,
    normed_in,
    gate_out,
    gate_in,
    reduce_bias_ref,
    counts_ref,
    count_in,
    chosen_out,
    chosen_in,
    rows_all,
    part_out,
    part_in,
    ret_out,
    ret_in,
    mix_out,
    mix_in,
    local_sem,
    head_send,
    head_recv,
    tok_send,
    tok_recv,
    frame_send,
    frame_recv,
):
    shards, heads, _, tokens = att_in.shape
    cols = heads * HD
    frames, slots = packs.shape[0], packs.shape[2]
    experts = gate_in.shape[1]
    frame_tokens = shards * tokens
    size = {"tok": shards, "frame": frames}
    me = {"tok": lax.axis_index("tok"), "frame": lax.axis_index("frame")}
    sems = {
        "tok": (tok_send, tok_recv),
        "frame": (frame_send, frame_recv),
        "head": (head_send, head_recv),
    }
    size["head"], me["head"] = size["tok"], me["tok"]
    real = {"tok": "tok", "frame": "frame", "head": "tok"}

    loads = [
        pltpu.make_async_copy(src, dst, local_sem.at[i])
        for i, (src, dst) in enumerate(((wo_hbm, wo), (we_hbm, we), (wr_hbm, wr)))
    ]
    for load in loads:
        load.start()

    barrier = pltpu.get_barrier_semaphore()
    for axis in ("tok", "frame"):
        for d in range(1, size[axis]):
            p = lax.rem(me[axis] + d, size[axis])
            pl.semaphore_signal(barrier, inc=1, device_id={axis: p}, device_id_type=MESH)
    pl.semaphore_wait(barrier, shards + frames - 2)

    def copy(axis, phase, src, dst, to, slot):
        send, recv = sems[axis]
        return pltpu.make_async_remote_copy(
            src_ref=src,
            dst_ref=dst.at[slot],
            send_sem=send.at[phase, to],
            recv_sem=recv.at[phase, slot],
            device_id={real[axis]: to},
            device_id_type=MESH,
        )

    sent = []

    def send_to(axis, phase, source, dst, d):
        p = lax.rem(me[axis] + d, size[axis])
        made = copy(axis, phase, source(p), dst, p, me[axis])
        made.start()
        sent.append(made)

    def send_all(axis, phase, source, dst):
        for d in range(1, size[axis]):
            send_to(axis, phase, source, dst, d)

    def take(axis, phase, source, dst, d):
        q = lax.rem(me[axis] + size[axis] - d, size[axis])
        copy(axis, phase, source(q), dst, q, q).wait_recv()
        return q

    def take_all(axis, phase, source, dst):
        for d in range(1, size[axis]):
            take(axis, phase, source, dst, d)

    tok, frame = me["tok"], me["frame"]
    for e in range(experts):
        counts_ref[e] = jnp.broadcast_to(own_counts_ref[e : e + 1, :], (8, 128))
    send_all("frame", 0, lambda p: counts_ref.at[p], count_in)
    count_in[frame] = counts_ref[frame]

    def part(t, h):
        return (t * heads + h, lambda p: qkv_out.at[t, p, h], qkv_in.at[t, :, h])

    for t, ref in enumerate((k_ref, q_ref, v_ref)):
        turned = ref[...].astype(F32).T
        for h in range(heads):
            for s in range(shards):
                base = s * cols + h * HD
                qkv_out[t, s, h] = turned[base : base + HD].astype(BF)
            if h == 0:
                send_all("head", *part(t, h))
    for h in range(1, heads):
        for t in range(3):
            send_all("head", *part(t, h))
    for t in range(3):
        qkv_in[t, tok] = qkv_out[t, tok]

    token = lax.broadcasted_iota(jnp.int32, (slots, frame_tokens), 1)
    for e in range(experts):
        used = lax.broadcasted_iota(jnp.int32, (1, slots), 1) < counts_ref[e][0:1, 0:slots]
        spot = jnp.where(used, picked_ref[e], -1).astype(F32)
        column = jnp.broadcast_to(spot, (128, slots)).T[:, 0:1].astype(jnp.int32)
        picks[e] = jnp.where(column == token, 1.0, 0.0).astype(BF)
    bias_columns = jnp.broadcast_to(reduce_bias_row[...], (8, shards * cols)).T
    for s in range(shards):
        reduce_bias_ref[s] = bias_columns[s * cols : (s + 1) * cols, 0:1]

    scale = math.log2(math.e) / math.sqrt(HD)
    for h in range(heads):
        for t in range(3):
            take_all("head", *part(t, h))
        keys = jnp.concatenate([qkv_in[0, s, h] for s in range(shards)], axis=1).T
        values = jnp.concatenate([qkv_in[2, s, h] for s in range(shards)], axis=1)

        def block(j, carry):
            scores = dot(keys, qkv_in[1, j, h], 1, 0)
            top = jnp.max(scores, axis=0, keepdims=True)
            powers = jnp.exp2((scores - top) * scale)
            denominator = jnp.sum(powers, axis=0, keepdims=True)
            out = dot(values, powers.astype(BF), 1, 0)
            att_out[j, h] = (out / denominator).astype(BF)
            return carry

        lax.fori_loop(0, shards, block, 0)
        send_all("head", 3 * heads + h, lambda p: att_out.at[p, h], att_in.at[:, h])
        att_in[tok, h] = att_out[tok, h]

    take_all("frame", 0, lambda p: counts_ref.at[p], count_in)
    row = lax.broadcasted_iota(jnp.int32, (CAP, slots), 0)
    slot = lax.broadcasted_iota(jnp.int32, (CAP, slots), 1)
    first = jnp.zeros((1, slots), jnp.int32)
    for g in range(frames):
        number = count_in[g][0:1, 0:slots]
        pack = jnp.where((row == first + slot) & (slot < number), 1.0, 0.0)
        packs[g] = pack.astype(BF)
        packs_turned[g] = pack.T.astype(BF)
        first = first + number
    loads[0].wait()

    def project(q):
        block = jnp.concatenate([att_in[q, h].astype(F32) for h in range(heads)], axis=0)
        return dot(block.T.astype(BF), wo[q], 1, 0)

    projected = project(tok)
    for d in range(1, shards):
        for h in range(heads):
            q = take("head", 3 * heads + h, lambda p: att_out.at[p, h], att_in.at[:, h], d)
        projected += project(q)
    projected += out_bias_ref[...].reshape(1, shards * cols)
    residual = (stream_ref[...].astype(F32) + mod_ref[0:1] * projected).astype(BF)
    wide = residual.astype(F32)
    centred = wide - jnp.mean(wide, axis=1, keepdims=True)
    variance = jnp.mean(centred * centred, axis=1, keepdims=True)
    normed = (
        centred * lax.rsqrt(variance + 1e-06) * (1.0 + mod_ref[2:3]) + mod_ref[1:2]
    ).astype(BF)
    turned = normed.T
    for s in range(shards):
        normed_out[s] = turned[s * cols : (s + 1) * cols]
    send_all("tok", 1, lambda p: normed_out.at[p], normed_in)
    o_ref[...] = residual
    gates = dot(router_ref[...], normed, 1, 1)
    gate_out[...] = 1.0 / (1.0 + jnp.exp(-gates))
    send_all("tok", 2, lambda p: gate_out, gate_in)
    normed_in[tok] = normed_out[tok]
    gate_in[tok] = gate_out[...]

    take_all("tok", 1, lambda p: normed_out.at[p], normed_in)
    held = jnp.concatenate([normed_in[s] for s in range(shards)], axis=1)
    for d in range(1, frames + 1):
        p = lax.rem(frame + d, frames)
        put_block(chosen_out, p, dot(picks[p], held, 1, 1), slots)
        if d < frames:
            send_to("frame", 1, lambda p: chosen_out.at[p], chosen_in, d)
    rows = dot(packs[frame], get_block(chosen_out, frame, slots, cols), 1, 0)
    for d in range(1, frames):
        g = take("frame", 1, lambda p: chosen_out.at[p], chosen_in, d)
        rows += dot(packs[g], get_block(chosen_in, g, slots, cols), 1, 0)
    rows_all[tok] = rows.T.astype(BF)
    send_all("tok", 3, lambda p: rows_all.at[tok], rows_all)
    loads[1].wait()
    loads[2].wait()
    hidden = dot(rows_all[tok].T, we[tok], 1, 0)
    for d in range(1, shards):
        q = take("tok", 3, lambda p: rows_all.at[tok], rows_all, d)
        hidden += dot(rows_all[q].T, we[q], 1, 0)
    hidden = gelu(hidden + expand_bias_ref[...]).astype(BF)
    partial_out = dot(hidden, wr[...], 1, 0).T
    for s in range(shards):
        part_out[s] = partial_out[s * cols : (s + 1) * cols].astype(BF)
    send_all("tok", 4, lambda p: part_out.at[p], part_in)
    part_in[tok] = part_out[tok]
    take_all("tok", 4, lambda p: part_out.at[p], part_in)
    total = part_in[0].astype(F32)
    for s in range(1, shards):
        total += part_in[s].astype(F32)
    expert_out = (total + reduce_bias_ref[tok]).astype(BF)
    for d in range(1, frames + 1):
        p = lax.rem(frame + d, frames)
        put_block(ret_out, p, dot(packs_turned[p], expert_out, 1, 1), slots)
        if d < frames:
            send_to("frame", 2, lambda p: ret_out.at[p], ret_in, d)
    take_all("tok", 2, lambda p: gate_out, gate_in)
    gate_all = jnp.concatenate([gate_in[s] for s in range(shards)], axis=1).astype(BF)
    for e in range(experts):
        picks[e] = picks[e] * gate_all[e : e + 1]
    mixed = dot(get_block(ret_out, frame, slots, cols).T, picks[frame], 1, 0)
    for d in range(1, frames):
        e = take("frame", 2, lambda p: ret_out.at[p], ret_in, d)
        mixed += dot(get_block(ret_in, e, slots, cols).T, picks[e], 1, 0)
    for s in range(shards):
        mix_out[s] = mixed[:, s * tokens : (s + 1) * tokens].astype(BF)
    send_all("tok", 5, lambda p: mix_out.at[p], mix_in)
    mix_in[tok] = mix_out[tok]
    take_all("tok", 5, lambda p: mix_out.at[p], mix_in)
    mix = jnp.concatenate([mix_in[s].astype(F32) for s in range(shards)], axis=0).T
    o_ref[...] = (o_ref[...].astype(F32) + mod_ref[3:4] * mix).astype(BF)
    for made in sent:
        made.wait_send()


def per_device(
    stream,
    queries,
    key_vectors,
    value_vectors,
    modulation,
    output_weight,
    output_bias,
    router_weight,
    expand_weight,
    expand_bias,
    reduce_weight,
    reduce_bias,
    counts,
    picked_rows,
):
    shards = lax.axis_size("tok")
    frames = lax.axis_size("frame")
    tokens = stream.shape[1]
    width = stream.shape[2]
    hidden = expand_weight.shape[2]
    cols = width // shards
    heads = H // shards
    experts, _, slots = picked_rows.shape

    vmem = pl.BlockSpec(memory_space=pltpu.VMEM)
    hbm = pl.BlockSpec(memory_space=pl.ANY)
    layer_out = pl.pallas_call(
        layer_kernel,
        out_shape=jax.ShapeDtypeStruct((tokens, width), BF),
        in_specs=[vmem] * 11 + [hbm] * 3,
        out_specs=vmem,
        scratch_shapes=[
            pltpu.VMEM((shards, cols, width), BF),
            pltpu.VMEM((shards, cols, hidden), BF),
            pltpu.VMEM((hidden, width), BF),
            pltpu.VMEM((3, shards, heads, HD, tokens), BF),
            pltpu.VMEM((3, shards, heads, HD, tokens), BF),
            pltpu.VMEM((shards, heads, HD, tokens), BF),
            pltpu.VMEM((shards, heads, HD, tokens), BF),
            pltpu.VMEM((experts, slots, shards * tokens), BF),
            pltpu.VMEM((frames, CAP, slots), BF),
            pltpu.VMEM((frames, slots, CAP), BF),
            pltpu.VMEM((shards, cols, tokens), BF),
            pltpu.VMEM((shards, cols, tokens), BF),
            pltpu.VMEM((experts, tokens), F32),
            pltpu.VMEM((shards, experts, tokens), F32),
            pltpu.VMEM((shards, cols, 1), F32),
            pltpu.VMEM((frames, 8, 128), jnp.int32),
            pltpu.VMEM((frames, 8, 128), jnp.int32),
            pltpu.VMEM((frames, *packed_shape(slots, cols)), BF),
            pltpu.VMEM((frames, *packed_shape(slots, cols)), BF),
            pltpu.VMEM((shards, cols, CAP), BF),
            pltpu.VMEM((shards, cols, CAP), BF),
            pltpu.VMEM((shards, cols, CAP), BF),
            pltpu.VMEM((frames, *packed_shape(slots, cols)), BF),
            pltpu.VMEM((frames, *packed_shape(slots, cols)), BF),
            pltpu.VMEM((shards, cols, tokens), BF),
            pltpu.VMEM((shards, cols, tokens), BF),
            pltpu.SemaphoreType.DMA((3,)),
            pltpu.SemaphoreType.DMA((4 * heads, shards)),
            pltpu.SemaphoreType.DMA((4 * heads, shards)),
            pltpu.SemaphoreType.DMA((6, shards)),
            pltpu.SemaphoreType.DMA((6, shards)),
            pltpu.SemaphoreType.DMA((3, frames)),
            pltpu.SemaphoreType.DMA((3, frames)),
        ],
        compiler_params=pltpu.CompilerParams(
            collective_id=1, has_side_effects=True, vmem_limit_bytes=56 << 20
        ),
    )(
        queries[0],
        key_vectors[0],
        value_vectors[0],
        stream[0],
        modulation[0],
        output_bias,
        router_weight.T,
        expand_bias,
        reduce_bias,
        counts,
        picked_rows,
        output_weight.reshape(shards, cols, width),
        expand_weight[0].reshape(shards, cols, hidden),
        reduce_weight[0],
    )
    return layer_out[None]


def solution(mesh):
    return jax.shard_map(
        per_device,
        mesh=mesh,
        in_specs=(
            P("frame", "tok", None),
            P("frame", "tok", None),
            P("frame", "tok", None),
            P("frame", "tok", None),
            P("frame", None, None),
            P(),
            P(),
            P(),
            P("frame", None, "tok"),
            P("frame", "tok"),
            P("frame", "tok", None),
            P("frame", None),
            P(None, "frame"),
            P(None, "frame", None),
        ),
        out_specs=P("frame", "tok", None),
        check_vma=False,
    )
```

profile of v0, /device:TPU:0, one launch (start us, length us, event | category | flops | bytes accessed | tf_op | source)
XLA Modules:
  0.0 96.7 jit_solution(11591478082246684720)
XLA Ops:
  0.0 1.3 %copy.15.own_counts_ref = s32[8,1]{1,0:T(8,128)} copy(s32[8,1]{0,1:T(1,128)} %param.26) | data formatting | bytes 64 | tf_op args[12]
  1.3 93.5 %shard_map.136 = bf16[256,1152]{1,0:T(8,128)(2,1)} custom-call(bf16[256,1152]{1,0:T(8,128)(2,1)} %bitcast.14, bf16[256,1152]{1,0:T(8,128)(2,1)} %bitcast.15, bf16[256,1152]{1,0:T(8,128)(2,1)} %bitcast.16, bf16[256,1152]{1,0:T(8,128)(2,1)} %bitcast.17, f32[4,1152]{1,0:T(4,128)} %bitcast.18, f32[1152]{0:T(1024)} %out_bias_ref.1, bf16[8,1152]{1,0:T(8,128)(2,1)} %bitcast.19, ...), custom_call_target="tpu_custom_call" | custom-call | tf_op jit(solution)/shard_map/pallas_call | solution.py:345
  94.8 1.9 %copy.17 = bf16[1,256,1152]{2,1,0:T(8,128)(2,1)} copy(bf16[1,256,1152]{2,1,0:T(8,128)(2,1)} %bitcast.13) | data formatting | bytes 1179648
where the time goes:
time: 96.9 us; the launch traced here: 96.7 us
  Pallas kernels  93.5 us (96%)
  local copies, waits for them, and re-layouts  3.24 us (3%)
    pallas_call x1, Pallas kernels, per_device(): pl.pallas_call(layer_kernel, out_shape=jax.ShapeDtypeStruct((tokens, widt...  93.5 us
    unnamed x2, local copies, waits for them, and re-layouts  3.24 us

commit v1 on v0

v1 whole, which is shorter than its diff:
```python
import math

import jax
import jax.numpy as jnp
from jax import lax
from jax.experimental import pallas as pl
from jax.experimental.pallas import tpu as pltpu
from jax.sharding import PartitionSpec as P

H = 16
HD = 72
CAP = 256
BF = jnp.bfloat16
F32 = jnp.float32


def dot(a, b, ca, cb):
    return lax.dot_general(a, b, (((ca,), (cb,)), ((), ())), preferred_element_type=F32)


MESH = pl.DeviceIdType.MESH


def gelu(x):
    return 0.5 * x * (1.0 + jnp.tanh(math.sqrt(2.0 / math.pi) * (x + 0.044715 * (x * x * x))))


LANES = 128


def packed_shape(slots, rest):
    if LANES % rest == 0 and slots % (LANES // rest) == 0 and slots * rest // LANES % 8 == 0:
        return (slots * rest // LANES, LANES)
    return (slots, rest)


def put_block(ref, at, x, slots):
    rest = x.shape[1]
    if ref.shape[1:] == (slots, rest):
        ref[at] = x.astype(BF)
        return
    high = slots * rest // LANES
    parts = [x[i * high : (i + 1) * high] for i in range(LANES // rest)]
    ref[at] = jnp.concatenate(parts, axis=1).astype(BF)


def get_block(ref, at, slots, rest):
    if ref.shape[1:] == (slots, rest):
        return ref[at].astype(F32)
    packed = ref[at].astype(F32)
    parts = [packed[:, i * rest : (i + 1) * rest] for i in range(LANES // rest)]
    return jnp.concatenate(parts, axis=0)


def partners(me, size):
    bits = size.bit_length() - 1
    if 1 << bits != size:
        return [lax.rem(me + d, size) for d in range(1, size)], [
            lax.rem(me + size - d, size) for d in range(1, size)
        ]
    digit = [lax.rem(lax.div(me, 1 << b), 2) for b in range(bits)]
    flipped = [
        sum((1 - digit[b] if d >> b & 1 else digit[b]) * (1 << b) for b in range(bits))
        for d in range(size - 1, 0, -1)
    ]
    return flipped, flipped


def layer_kernel(
    q_ref,
    k_ref,
    v_ref,
    stream_ref,
    mod_ref,
    out_bias_ref,
    router_ref,
    expand_bias_ref,
    reduce_bias_row,
    own_counts_ref,
    picked_ref,
    wo_hbm,
    we_hbm,
    wr_hbm,
    o_ref,
    wo,
    we,
    wr,
    qkv_out,
    qkv_in,
    att_out,
    att_in,
    picks,
    mixers,
    packs,
    packs_turned,
    gate_out,
    gate_in,
    bias_tiles,
    bias_columns,
    counts_ref,
    count_in,
    wide_bufs,
    rest_bufs,
    local_sem,
    head_send,
    head_recv,
    tok_send,
    tok_recv,
    frame_send,
    frame_recv,
):
    shards, heads, _, tokens = att_in.shape
    cols = heads * HD
    full, rest = cols // LANES, cols % LANES
    frames = count_in.shape[0]
    experts = gate_in.shape[1]
    slots = picks.shape[0] // experts
    frame_tokens = shards * tokens
    size = {"tok": shards, "frame": frames}
    me = {"tok": lax.axis_index("tok"), "frame": lax.axis_index("frame")}
    sems = {
        "tok": (tok_send, tok_recv),
        "frame": (frame_send, frame_recv),
        "head": (head_send, head_recv),
    }
    size["head"], me["head"] = size["tok"], me["tok"]
    real = {"tok": "tok", "frame": "frame", "head": "tok"}
    to = {axis: partners(me[axis], size[axis]) for axis in ("tok", "frame")}
    to["head"] = to["tok"]
    tok, frame = me["tok"], me["frame"]

    barrier = pltpu.get_barrier_semaphore()
    for axis in ("frame", "tok"):
        for p in to[axis][0]:
            pl.semaphore_signal(barrier, inc=1, device_id={axis: p}, device_id_type=MESH)

    loads = [
        pltpu.make_async_copy(src, dst, local_sem.at[i])
        for i, (src, dst) in enumerate(((wo_hbm, wo), (we_hbm, we), (wr_hbm, wr)))
    ]
    for load in loads:
        load.start()

    def copy(axis, phase, src, dst, to, slot):
        send, recv = sems[axis]
        return pltpu.make_async_remote_copy(
            src_ref=src,
            dst_ref=dst.at[slot],
            send_sem=send.at[phase, to],
            recv_sem=recv.at[phase, slot],
            device_id={real[axis]: to},
            device_id_type=MESH,
        )

    sent = []

    def send_to(axis, phase, source, dst, p):
        made = copy(axis, phase, source(p), dst, p, me[axis])
        made.start()
        sent.append(made)

    def send_all(axis, phase, source, dst):
        for p in to[axis][0]:
            send_to(axis, phase, source, dst, p)

    def take(axis, phase, source, dst, q):
        copy(axis, phase, source(q), dst, q, q).wait_recv()

    def take_all(axis, phase, source, dst):
        for q in to[axis][1]:
            take(axis, phase, source, dst, q)

    for e in range(experts):
        counts_ref[e] = jnp.broadcast_to(own_counts_ref[:, e : e + 1], (8, 128))
    count_in[frame] = counts_ref[frame]

    def part(t, h):
        return (t * heads + h, lambda p: qkv_out.at[t, p, h], qkv_in.at[t, :, h])

    for t, ref in enumerate((k_ref, v_ref, q_ref)):
        turned = ref[...].astype(F32).T
        for h in range(heads):
            for s in range(shards):
                base = s * cols + h * HD
                qkv_out[t, s, h] = turned[base : base + HD].astype(BF)
    pl.semaphore_wait(barrier, shards + frames - 2)
    for h in range(heads):
        for t in range(3):
            send_all("head", *part(t, h))
    send_all("frame", 0, lambda p: counts_ref.at[p], count_in)
    for t in range(3):
        qkv_in[t, tok] = qkv_out[t, tok]

    token = lax.broadcasted_iota(jnp.int32, (slots, frame_tokens), 1)
    spots = []
    for e in range(experts):
        used = lax.broadcasted_iota(jnp.int32, (1, slots), 1) < counts_ref[e][0:1, 0:slots]
        spot = jnp.where(used, picked_ref[e], -1)
        column = jnp.broadcast_to(spot.astype(F32), (128, slots)).T[:, 0:1].astype(jnp.int32)
        picks[e * slots : (e + 1) * slots] = jnp.where(column == token, 1.0, 0.0).astype(BF)
        spots.append(spot)
    spots = jnp.concatenate(spots, axis=1)
    for s in range(shards):
        token = lax.broadcasted_iota(jnp.int32, (tokens, experts * slots), 0) + s * tokens
        mixers[s] = jnp.where(spots == token, 1.0, 0.0).astype(BF)
    for i in range(full):
        for s in range(shards):
            base = (i * shards + s) * LANES
            bias_tiles[i, s] = jnp.broadcast_to(reduce_bias_row[:, base : base + LANES], (8, LANES))
    wide = full * shards * LANES
    if rest:
        turned = jnp.broadcast_to(reduce_bias_row[:, wide:], (8, shards * rest)).T
        for s in range(shards):
            bias_columns[s] = turned[s * rest : (s + 1) * rest, 0:1]

    scale = math.log2(math.e) / math.sqrt(HD)
    for h in range(heads):
        for t in range(2):
            take_all("head", *part(t, h))
        keys = jnp.concatenate([qkv_in[0, s, h] for s in range(shards)], axis=1).T
        values = jnp.concatenate([qkv_in[1, s, h] for s in range(shards)], axis=1)

        def block(i, carry):
            j = lax.rem(tok + i, shards)

            @pl.when(i > 0)
            def _():
                take("head", *part(2, h), j)

            scores = dot(keys, qkv_in[2, j, h], 1, 0)
            top = jnp.max(scores, axis=0, keepdims=True)
            powers = jnp.exp2((scores - top) * scale)
            denominator = jnp.sum(powers, axis=0, keepdims=True)
            out = dot(values, powers.astype(BF), 1, 0)
            att_out[j, h] = (out / denominator).astype(BF)

            @pl.when(i > 0)
            def _():
                copy("head", 3 * heads + h, att_out.at[j, h], att_in.at[:, h], j, tok).start()

            return carry

        lax.fori_loop(0, shards, block, 0)
        att_in[tok, h] = att_out[tok, h]
        sent.extend(
            copy("head", 3 * heads + h, att_out.at[p, h], att_in.at[:, h], p, tok)
            for p in to["head"][0]
        )

    take_all("frame", 0, lambda p: counts_ref.at[p], count_in)
    slot = lax.broadcasted_iota(jnp.int32, (1, slots), 1)
    turned_row = lax.broadcasted_iota(jnp.int32, (slots, CAP), 1)
    turned_slot = lax.broadcasted_iota(jnp.int32, (slots, CAP), 0)
    first = jnp.zeros((1, LANES), jnp.int32)
    targets = []
    for g in range(frames):
        number = count_in[g][0:1]
        targets.append(jnp.where(slot < number[:, 0:slots], first[:, 0:slots] + slot, -1))
        high = jnp.concatenate([number] * (CAP // LANES), axis=1)
        low = jnp.concatenate([first] * (CAP // LANES), axis=1)
        chosen = (turned_row == low + turned_slot) & (turned_slot < high)
        packs_turned[g * slots : (g + 1) * slots] = jnp.where(chosen, 1.0, 0.0).astype(BF)
        first = first + number
    row = lax.broadcasted_iota(jnp.int32, (CAP, frames * slots), 0)
    packs[...] = jnp.where(row == jnp.concatenate(targets, axis=1), 1.0, 0.0).astype(BF)
    loads[0].wait()

    def project(q):
        block = jnp.concatenate([att_in[q, h].astype(F32) for h in range(heads)], axis=0)
        return dot(block.T.astype(BF), wo[q], 1, 0)

    projected = project(tok)
    for q in to["head"][1]:
        for h in range(heads):
            take("head", 3 * heads + h, lambda p: att_out.at[p, h], att_in.at[:, h], q)
        projected += project(q)
    projected += out_bias_ref[...].reshape(1, shards * cols)
    residual = (stream_ref[...].astype(F32) + mod_ref[0:1] * projected).astype(BF)
    o_ref[...] = residual
    residual = residual.astype(F32)
    centred = residual - jnp.mean(residual, axis=1, keepdims=True)
    variance = jnp.mean(centred * centred, axis=1, keepdims=True)
    normed = (
        centred * lax.rsqrt(variance + 1e-06) * (1.0 + mod_ref[2:3]) + mod_ref[1:2]
    ).astype(BF)

    normed_out, normed_in, chosen_out, chosen_in, rows_all, part_out, part_in = wide_bufs[:7]
    ret_out, ret_in, mix_out, mix_in = wide_bufs[7:]
    slim_normed_out, slim_normed_in, slim_chosen_out, slim_chosen_in = rest_bufs[:4]
    slim_rows, slim_part_out, slim_part_in, slim_ret_out, slim_ret_in = rest_bufs[4:9]
    slim_mix_out, slim_mix_in = rest_bufs[9:]
    chunks = list(range(full)) + [full] * (rest > 0)
    steps = full + 1

    def chunk(axis, stage, i, wide_from, wide_to, slim_from, slim_to):
        phase = 1 + stage * steps + i
        if i < full:
            return (axis, phase, lambda p: wide_from.at[i, p], wide_to.at[i])
        return (axis, phase, lambda p: slim_from.at[p], slim_to)

    def normed_of(i):
        return chunk("tok", 0, i, normed_out, normed_in, slim_normed_out, slim_normed_in)

    def chosen_of(i):
        return chunk("frame", 0, i, chosen_out, chosen_in, slim_chosen_out, slim_chosen_in)

    def rows_of(i):
        if i < full:
            return ("tok", 1 + steps + i, lambda p: rows_all.at[i, tok], rows_all.at[i])
        return ("tok", 1 + steps + i, lambda p: slim_rows.at[tok], slim_rows)

    def part_of(i):
        return chunk("tok", 2, i, part_out, part_in, slim_part_out, slim_part_in)

    def ret_of(i):
        return chunk("frame", 1, i, ret_out, ret_in, slim_ret_out, slim_ret_in)

    def mix_of(i):
        return chunk("tok", 3, i, mix_out, mix_in, slim_mix_out, slim_mix_in)

    def stacked(ref):
        n, high = ref.shape[0], ref.shape[1]
        if high % 16 == 0:
            return jnp.concatenate([ref[s] for s in range(n)], axis=0)
        return jnp.concatenate([ref[s].astype(F32) for s in range(n)], axis=0).astype(BF)

    def unpacked(ref):
        blocks = [get_block(ref, g, slots, rest) for g in range(ref.shape[0])]
        return jnp.concatenate(blocks, axis=0).astype(BF)

    for i in chunks:
        if i < full:
            for s in range(shards):
                base = (i * shards + s) * LANES
                normed_out[i, s] = normed[:, base : base + LANES]
        else:
            turned = normed[:, wide:].T
            for s in range(shards):
                slim_normed_out[s] = turned[s * rest : (s + 1) * rest]
        send_all(*normed_of(i))
    gates = dot(router_ref[...], normed, 1, 1)
    gate_out[...] = 1.0 / (1.0 + jnp.exp(-gates))
    send_all("tok", 0, lambda p: gate_out, gate_in)
    gate_in[tok] = gate_out[...]

    for i in chunks:
        if i < full:
            normed_in[i, tok] = normed_out[i, tok]
            take_all(*normed_of(i))
            held = normed_in[i].reshape(frame_tokens, LANES)
            chosen = dot(picks[...], held, 1, 0)
            for e in range(experts):
                chosen_out[i, e] = chosen[e * slots : (e + 1) * slots].astype(BF)
            send_all(*chosen_of(i))
            chosen_in[i, frame] = chosen_out[i, frame]
        else:
            slim_normed_in[tok] = slim_normed_out[tok]
            take_all(*normed_of(i))
            held = jnp.concatenate([slim_normed_in[s] for s in range(shards)], axis=1)
            chosen = dot(picks[...], held, 1, 1)
            for e in range(experts):
                put_block(slim_chosen_out, e, chosen[e * slots : (e + 1) * slots], slots)
            send_all(*chosen_of(i))
            slim_chosen_in[frame] = slim_chosen_out[frame]

    take_all("tok", 0, lambda p: gate_out, gate_in)
    owner = lax.broadcasted_iota(jnp.int32, (experts, experts * slots), 1)
    expert = lax.broadcasted_iota(jnp.int32, (experts, experts * slots), 0) * slots
    spread = jnp.where((owner >= expert) & (owner < expert + slots), 1.0, 0.0).astype(BF)
    for s in range(shards):
        mixers[s] = mixers[s] * dot(gate_in[s].astype(BF), spread, 0, 0).astype(BF)

    loads[1].wait()
    hidden = None

    def expand(i, hidden):
        take_all(*rows_of(i))
        if i < full:
            base = i * shards * LANES
            rows = jnp.concatenate([rows_all[i, s] for s in range(shards)], axis=1)
            more = dot(rows, we[base : base + shards * LANES], 1, 0)
        else:
            more = dot(stacked(slim_rows), we[wide:], 0, 0)
        return more if hidden is None else hidden + more

    for at, i in enumerate(chunks):
        take_all(*chosen_of(i))
        if i < full:
            rows = dot(packs[...], chosen_in[i].reshape(frames * slots, LANES), 1, 0)
            rows_all[i, tok] = rows.astype(BF)
        else:
            slim_rows[tok] = dot(packs[...], unpacked(slim_chosen_in), 1, 0).T.astype(BF)
        send_all(*rows_of(i))
        if at:
            hidden = expand(chunks[at - 1], hidden)
    hidden = expand(chunks[-1], hidden)
    hidden = gelu(hidden + expand_bias_ref[...]).astype(BF)
    loads[2].wait()

    for i in chunks:
        if i < full:
            base = i * shards * LANES
            out = dot(hidden, wr[:, base : base + shards * LANES], 1, 0)
            for s in range(shards):
                part_out[i, s] = out[:, s * LANES : (s + 1) * LANES].astype(BF)
        else:
            out = dot(hidden, wr[:, wide:], 1, 0).T
            for s in range(shards):
                slim_part_out[s] = out[s * rest : (s + 1) * rest].astype(BF)
        send_all(*part_of(i))
    for i in chunks:
        if i < full:
            part_in[i, tok] = part_out[i, tok]
            take_all(*part_of(i))
            total = part_in[i, 0].astype(F32)
            for s in range(1, shards):
                total += part_in[i, s].astype(F32)
            out = (total + bias_tiles[i, tok][0:1]).astype(BF)
            back = dot(packs_turned[...], out, 1, 0)
            for g in range(frames):
                ret_out[i, g] = back[g * slots : (g + 1) * slots].astype(BF)
            send_all(*ret_of(i))
            ret_in[i, frame] = ret_out[i, frame]
        else:
            slim_part_in[tok] = slim_part_out[tok]
            take_all(*part_of(i))
            total = slim_part_in[0].astype(F32)
            for s in range(1, shards):
                total += slim_part_in[s].astype(F32)
            out = (total + bias_columns[tok]).astype(BF)
            back = dot(packs_turned[...], out, 1, 1)
            for g in range(frames):
                put_block(slim_ret_out, g, back[g * slots : (g + 1) * slots], slots)
            send_all(*ret_of(i))
            slim_ret_in[frame] = slim_ret_out[frame]

    for i in chunks:
        take_all(*ret_of(i))
        if i < full:
            back = ret_in[i].reshape(experts * slots, LANES)
            for p in to["tok"][0]:
                mix_out[i, p] = dot(mixers[p], back, 1, 0).astype(BF)
                send_to(*mix_of(i), p)
            mix_in[i, tok] = dot(mixers[tok], back, 1, 0).astype(BF)
        else:
            back = unpacked(slim_ret_in)
            for p in to["tok"][0]:
                slim_mix_out[p] = dot(mixers[p], back, 1, 0).T.astype(BF)
                send_to(*mix_of(i), p)
            slim_mix_in[tok] = dot(mixers[tok], back, 1, 0).T.astype(BF)
    for i in chunks:
        take_all(*mix_of(i))
        if i < full:
            for s in range(shards):
                base = (i * shards + s) * LANES
                at = slice(base, base + LANES)
                mix = mix_in[i, s].astype(F32)
                o_ref[:, at] = (o_ref[:, at].astype(F32) + mod_ref[3:4, at] * mix).astype(BF)
        else:
            mix = stacked(slim_mix_in).astype(F32).T
            at = slice(wide, wide + shards * rest)
            o_ref[:, at] = (o_ref[:, at].astype(F32) + mod_ref[3:4, at] * mix).astype(BF)
    for made in sent:
        made.wait_send()


def per_device(
    stream,
    queries,
    key_vectors,
    value_vectors,
    modulation,
    output_weight,
    output_bias,
    router_weight,
    expand_weight,
    expand_bias,
    reduce_weight,
    reduce_bias,
    counts,
    picked_rows,
):
    shards = lax.axis_size("tok")
    frames = lax.axis_size("frame")
    tokens = stream.shape[1]
    width = stream.shape[2]
    hidden = expand_weight.shape[2]
    cols = width // shards
    heads = H // shards
    experts, _, slots = picked_rows.shape
    full, rest = cols // LANES, cols % LANES
    wide, slim = max(full, 1), max(rest, 8)
    steps = full + 1

    vmem = pl.BlockSpec(memory_space=pltpu.VMEM)
    hbm = pl.BlockSpec(memory_space=pl.ANY)
    by_token = pltpu.VMEM((wide, shards, tokens, LANES), BF)
    by_frame = pltpu.VMEM((wide, frames, slots, LANES), BF)
    by_row = pltpu.VMEM((wide, shards, CAP, LANES), BF)
    slim_token = pltpu.VMEM((shards, slim, tokens), BF)
    slim_frame = pltpu.VMEM((frames, *packed_shape(slots, slim)), BF)
    slim_row = pltpu.VMEM((shards, slim, CAP), BF)
    layer_out = pl.pallas_call(
        layer_kernel,
        out_shape=jax.ShapeDtypeStruct((tokens, width), BF),
        in_specs=[vmem] * 11 + [hbm] * 3,
        out_specs=vmem,
        scratch_shapes=[
            pltpu.VMEM((shards, cols, width), BF),
            pltpu.VMEM((width, hidden), BF),
            pltpu.VMEM((hidden, width), BF),
            pltpu.VMEM((3, shards, heads, HD, tokens), BF),
            pltpu.VMEM((3, shards, heads, HD, tokens), BF),
            pltpu.VMEM((shards, heads, HD, tokens), BF),
            pltpu.VMEM((shards, heads, HD, tokens), BF),
            pltpu.VMEM((experts * slots, shards * tokens), BF),
            pltpu.VMEM((shards, tokens, experts * slots), BF),
            pltpu.VMEM((CAP, frames * slots), BF),
            pltpu.VMEM((frames * slots, CAP), BF),
            pltpu.VMEM((experts, tokens), F32),
            pltpu.VMEM((shards, experts, tokens), F32),
            pltpu.VMEM((wide, shards, 8, LANES), F32),
            pltpu.VMEM((shards, slim, 1), F32),
            pltpu.VMEM((frames, 8, 128), jnp.int32),
            pltpu.VMEM((frames, 8, 128), jnp.int32),
            [by_token] * 2 + [by_frame] * 2 + [by_row] * 3 + [by_frame] * 2 + [by_token] * 2,
            [slim_token] * 2 + [slim_frame] * 2 + [slim_row] * 3 + [slim_frame] * 2 + [slim_token] * 2,
            pltpu.SemaphoreType.DMA((3,)),
            pltpu.SemaphoreType.DMA((4 * heads, shards)),
            pltpu.SemaphoreType.DMA((4 * heads, shards)),
            pltpu.SemaphoreType.DMA((1 + 4 * steps, shards)),
            pltpu.SemaphoreType.DMA((1 + 4 * steps, shards)),
            pltpu.SemaphoreType.DMA((1 + 2 * steps, frames)),
            pltpu.SemaphoreType.DMA((1 + 2 * steps, frames)),
        ],
        compiler_params=pltpu.CompilerParams(
            collective_id=1, has_side_effects=True, vmem_limit_bytes=60 << 20
        ),
    )(
        queries[0],
        key_vectors[0],
        value_vectors[0],
        stream[0],
        modulation[0],
        output_bias,
        router_weight.T,
        expand_bias,
        reduce_bias,
        counts.T,
        picked_rows,
        output_weight.reshape(shards, cols, width),
        expand_weight[0],
        reduce_weight[0],
    )
    return layer_out[None]


def solution(mesh):
    return jax.shard_map(
        per_device,
        mesh=mesh,
        in_specs=(
            P("frame", "tok", None),
            P("frame", "tok", None),
            P("frame", "tok", None),
            P("frame", "tok", None),
            P("frame", None, None),
            P(),
            P(),
            P(),
            P("frame", None, "tok"),
            P("frame", "tok"),
            P("frame", "tok", None),
            P("frame", None),
            P(None, "frame"),
            P(None, "frame", None),
        ),
        out_specs=P("frame", "tok", None),
        check_vma=False,
    )
```

time: 96.9 us -> 87.4 us (0.902)
  Pallas kernels: 93.5 us -> 85.3 us
  local copies, waits for them, and re-layouts: 3.24 us -> 1.92 us
    pallas_call x1, Pallas kernels: 93.5 us -> 85.3 us  [per_device(): pl.pallas_call(layer_kernel, out_shape=jax.ShapeDtypeStruct((tokens, widt...]
    unnamed x2 -> x1, local copies, waits for them, and re-layouts: 3.24 us -> 1.92 us
where the time goes in v1:
time: 87.4 us; the launch traced here: 87.2 us
  Pallas kernels  85.3 us (98%)
  local copies, waits for them, and re-layouts  1.92 us (2%)
    pallas_call x1, Pallas kernels, per_device(): pl.pallas_call(layer_kernel, out_shape=jax.ShapeDtypeStruct((tokens, widt...  85.3 us
    unnamed x1, local copies, waits for them, and re-layouts  1.92 us

profile of v1, /device:TPU:0, one launch (start us, length us, event | category | flops | bytes accessed | tf_op | source)
XLA Modules:
  0.0 87.2 jit_solution(11872526932622740079)
XLA Ops:
  0.0 85.3 %shard_map.136 = bf16[256,1152]{1,0:T(8,128)(2,1)} custom-call(bf16[256,1152]{1,0:T(8,128)(2,1)} %bitcast.15, bf16[256,1152]{1,0:T(8,128)(2,1)} %bitcast.16, bf16[256,1152]{1,0:T(8,128)(2,1)} %bitcast.17, bf16[256,1152]{1,0:T(8,128)(2,1)} %bitcast.18, f32[4,1152]{1,0:T(4,128)} %bitcast.19, f32[1152]{0:T(1024)} %out_bias_ref.1, bf16[8,1152]{1,0:T(8,128)(2,1)} %bitcast.20, ...), custom_call_target="tpu_custom_call" | custom-call | tf_op jit(solution)/shard_map/pallas_call | solution.py:503
  85.3 1.9 %copy.16 = bf16[1,256,1152]{2,1,0:T(8,128)(2,1)} copy(bf16[1,256,1152]{2,1,0:T(8,128)(2,1)} %bitcast.14) | data formatting | bytes 1179648

commit v2 on v1

--- a/solution.py
+++ b/solution.py
@@ -67,48 +67,53 @@
 
 
 def layer_kernel(
-    q_ref,
-    k_ref,
-    v_ref,
-    stream_ref,
-    mod_ref,
-    out_bias_ref,
-    router_ref,
-    expand_bias_ref,
-    reduce_bias_row,
-    own_counts_ref,
-    picked_ref,
-    wo_hbm,
-    we_hbm,
-    wr_hbm,
-    o_ref,
-    wo,
-    we,
-    wr,
-    qkv_out,
-    qkv_in,
-    att_out,
-    att_in,
-    picks,
-    mixers,
-    packs,
-    packs_turned,
-    gate_out,
-    gate_in,
-    bias_tiles,
-    bias_columns,
-    counts_ref,
-    count_in,
-    wide_bufs,
-    rest_bufs,
-    local_sem,
-    head_send,
-    head_recv,
-    tok_send,
-    tok_recv,
-    frame_send,
-    frame_recv,
+    *refs,
 ):
+    sources, o_ref, held_inputs = refs[:14], refs[14], refs[15:29]
+    (
+        q_ref,
+        k_ref,
+        v_ref,
+        stream_ref,
+        mod_ref,
+        out_bias_ref,
+        router_ref,
+        expand_bias_ref,
+        reduce_bias_row,
+        own_counts_ref,
+        picked_ref,
+        wo,
+        we,
+        wr,
+    ) = held_inputs
+    (
+        qkv_out,
+        qkv_in,
+        att_out,
+        att_in,
+        picks,
+        mixers,
+        packs,
+        packs_turned,
+        gate_out,
+        gate_in,
+        bias_tiles,
+        bias_columns,
+        counts_ref,
+        count_in,
+        wide_bufs,
+        rest_bufs,
+        local_sem,
+        qkv_send,
+        kv_recv,
+        q_recv,
+        att_send,
+        att_recv,
+        tok_send,
+        tok_recv,
+        frame_send,
+        frame_recv,
+    ) = refs[29:]
     shards, heads, _, tokens = att_in.shape
     cols = heads * HD
     full, rest = cols // LANES, cols % LANES
@@ -118,15 +123,8 @@
     frame_tokens = shards * tokens
     size = {"tok": shards, "frame": frames}
     me = {"tok": lax.axis_index("tok"), "frame": lax.axis_index("frame")}
-    sems = {
-        "tok": (tok_send, tok_recv),
-        "frame": (frame_send, frame_recv),
-        "head": (head_send, head_recv),
-    }
-    size["head"], me["head"] = size["tok"], me["tok"]
-    real = {"tok": "tok", "frame": "frame", "head": "tok"}
+    sems = {"tok": (tok_send, tok_recv), "frame": (frame_send, frame_recv)}
     to = {axis: partners(me[axis], size[axis]) for axis in ("tok", "frame")}
-    to["head"] = to["tok"]
     tok, frame = me["tok"], me["frame"]
 
     barrier = pltpu.get_barrier_semaphore()
@@ -136,48 +134,47 @@
 
     loads = [
         pltpu.make_async_copy(src, dst, local_sem.at[i])
-        for i, (src, dst) in enumerate(((wo_hbm, wo), (we_hbm, we), (wr_hbm, wr)))
+        for i, (src, dst) in enumerate(zip(sources, held_inputs))
     ]
-    for load in loads:
-        load.start()
-
-    def copy(axis, phase, src, dst, to, slot):
-        send, recv = sems[axis]
+    for i in (1, 2, 0, 9, 10, 8, 3, 4, 5, 6, 7, 11, 12, 13):
+        loads[i].start()
+
+    def remote(src, dst, send_sem, recv_sem, axis, p):
         return pltpu.make_async_remote_copy(
             src_ref=src,
-            dst_ref=dst.at[slot],
-            send_sem=send.at[phase, to],
-            recv_sem=recv.at[phase, slot],
-            device_id={real[axis]: to},
+            dst_ref=dst,
+            send_sem=send_sem,
+            recv_sem=recv_sem,
+            device_id={axis: p},
             device_id_type=MESH,
         )
 
-    sent = []
+    unsent = []
+
+    def sends_of(ref, sem, axis):
+        unsent.append(remote(ref, ref, sem, sem, axis, me[axis]))
 
     def send_to(axis, phase, source, dst, p):
-        made = copy(axis, phase, source(p), dst, p, me[axis])
-        made.start()
-        sent.append(made)
+        send, recv = sems[axis]
+        remote(source(p), dst.at[me[axis]], send.at[phase], recv.at[phase], axis, p).start()
 
     def send_all(axis, phase, source, dst):
         for p in to[axis][0]:
             send_to(axis, phase, source, dst, p)
 
-    def take(axis, phase, source, dst, q):
-        copy(axis, phase, source(q), dst, q, q).wait_recv()
-
     def take_all(axis, phase, source, dst):
-        for q in to[axis][1]:
-            take(axis, phase, source, dst, q)
-
+        send, recv = sems[axis]
+        come = dst.at[0 : size[axis] - 1]
+        remote(come, come, send.at[phase], recv.at[phase], axis, me[axis]).wait_recv()
+        sends_of(come, send.at[phase], axis)
+
+    loads[9].wait()
     for e in range(experts):
         counts_ref[e] = jnp.broadcast_to(own_counts_ref[:, e : e + 1], (8, 128))
     count_in[frame] = counts_ref[frame]
 
-    def part(t, h):
-        return (t * heads + h, lambda p: qkv_out.at[t, p, h], qkv_in.at[t, :, h])
-
     for t, ref in enumerate((k_ref, v_ref, q_ref)):
+        loads[(1, 2, 0)[t]].wait()
         turned = ref[...].astype(F32).T
         for h in range(heads):
             for s in range(shards):
@@ -186,11 +183,17 @@
     pl.semaphore_wait(barrier, shards + frames - 2)
     for h in range(heads):
         for t in range(3):
-            send_all("head", *part(t, h))
+            recv = (q_recv if t == 2 else kv_recv).at[h]
+            for p in to["tok"][0]:
+                remote(
+                    qkv_out.at[t, p, h], qkv_in.at[t, tok, h], qkv_send.at[0], recv, "tok", p
+                ).start()
     send_all("frame", 0, lambda p: counts_ref.at[p], count_in)
     for t in range(3):
         qkv_in[t, tok] = qkv_out[t, tok]
 
+    loads[10].wait()
+    loads[8].wait()
     token = lax.broadcasted_iota(jnp.int32, (slots, frame_tokens), 1)
     spots = []
     for e in range(experts):
@@ -214,18 +217,30 @@
             bias_columns[s] = turned[s * rest : (s + 1) * rest, 0:1]
 
     scale = math.log2(math.e) / math.sqrt(HD)
+    others = shards - 1
+
+    def far(i):
+        if 1 << shards.bit_length() - 1 != shards:
+            return lax.rem(tok + i, shards)
+        flip, p = lax.rem(shards - i, shards), 0
+        for b in range(shards.bit_length() - 1):
+            mine, turn = (lax.rem(lax.div(x, 1 << b), 2) for x in (tok, flip))
+            p += (mine + turn - 2 * mine * turn) * (1 << b)
+        return p
+
     for h in range(heads):
-        for t in range(2):
-            take_all("head", *part(t, h))
+        come = qkv_in.at[0:2, 0:others, h]
+        remote(come, come, qkv_send.at[0], kv_recv.at[h], "tok", tok).wait_recv()
         keys = jnp.concatenate([qkv_in[0, s, h] for s in range(shards)], axis=1).T
         values = jnp.concatenate([qkv_in[1, s, h] for s in range(shards)], axis=1)
 
         def block(i, carry):
-            j = lax.rem(tok + i, shards)
-
-            @pl.when(i > 0)
+            j = far(i)
+
+            @pl.when(i == 1)
             def _():
-                take("head", *part(2, h), j)
+                come = qkv_in.at[2, 0:others, h]
+                remote(come, come, qkv_send.at[0], q_recv.at[h], "tok", tok).wait_recv()
 
             scores = dot(keys, qkv_in[2, j, h], 1, 0)
             top = jnp.max(scores, axis=0, keepdims=True)
@@ -236,16 +251,21 @@
 
             @pl.when(i > 0)
             def _():
-                copy("head", 3 * heads + h, att_out.at[j, h], att_in.at[:, h], j, tok).start()
+                remote(
+                    att_out.at[j, h],
+                    att_in.at[tok, h],
+                    att_send.at[0],
+                    att_recv.at[tok],
+                    "tok",
+                    j,
+                ).start()
 
             return carry
 
         lax.fori_loop(0, shards, block, 0)
         att_in[tok, h] = att_out[tok, h]
-        sent.extend(
-            copy("head", 3 * heads + h, att_out.at[p, h], att_in.at[:, h], p, tok)
-            for p in to["head"][0]
-        )
+    sends_of(qkv_out.at[:, 0:others], qkv_send.at[0], "tok")
+    sends_of(att_out.at[0:others], att_send.at[0], "tok")
 
     take_all("frame", 0, lambda p: counts_ref.at[p], count_in)
     slot = lax.broadcasted_iota(jnp.int32, (1, slots), 1)
@@ -263,17 +283,20 @@
         first = first + number
     row = lax.broadcasted_iota(jnp.int32, (CAP, frames * slots), 0)
     packs[...] = jnp.where(row == jnp.concatenate(targets, axis=1), 1.0, 0.0).astype(BF)
-    loads[0].wait()
+    loads[11].wait()
 
     def project(q):
         block = jnp.concatenate([att_in[q, h].astype(F32) for h in range(heads)], axis=0)
         return dot(block.T.astype(BF), wo[q], 1, 0)
 
     projected = project(tok)
-    for q in to["head"][1]:
-        for h in range(heads):
-            take("head", 3 * heads + h, lambda p: att_out.at[p, h], att_in.at[:, h], q)
+    for q in to["tok"][1][::-1]:
+        remote(
+            att_in.at[q], att_in.at[q], att_send.at[0], att_recv.at[q], "tok", tok
+        ).wait_recv()
         projected += project(q)
+    for i in (3, 4, 5, 6):
+        loads[i].wait()
     projected += out_bias_ref[...].reshape(1, shards * cols)
     residual = (stream_ref[...].astype(F32) + mod_ref[0:1] * projected).astype(BF)
     o_ref[...] = residual
@@ -370,7 +393,8 @@
     for s in range(shards):
         mixers[s] = mixers[s] * dot(gate_in[s].astype(BF), spread, 0, 0).astype(BF)
 
-    loads[1].wait()
+    loads[12].wait()
+    loads[7].wait()
     hidden = None
 
     def expand(i, hidden):
@@ -383,7 +407,7 @@
             more = dot(stacked(slim_rows), we[wide:], 0, 0)
         return more if hidden is None else hidden + more
 
-    for at, i in enumerate(chunks):
+    for i in chunks:
         take_all(*chosen_of(i))
         if i < full:
             rows = dot(packs[...], chosen_in[i].reshape(frames * slots, LANES), 1, 0)
@@ -391,11 +415,10 @@
         else:
             slim_rows[tok] = dot(packs[...], unpacked(slim_chosen_in), 1, 0).T.astype(BF)
         send_all(*rows_of(i))
-        if at:
-            hidden = expand(chunks[at - 1], hidden)
-    hidden = expand(chunks[-1], hidden)
+    for i in chunks:
+        hidden = expand(i, hidden)
     hidden = gelu(hidden + expand_bias_ref[...]).astype(BF)
-    loads[2].wait()
+    loads[13].wait()
 
     for i in chunks:
         if i < full:
@@ -460,7 +483,7 @@
             mix = stacked(slim_mix_in).astype(F32).T
             at = slice(wide, wide + shards * rest)
             o_ref[:, at] = (o_ref[:, at].astype(F32) + mod_ref[3:4, at] * mix).astype(BF)
-    for made in sent:
+    for made in unsent:
         made.wait_send()
 
 
@@ -500,15 +523,29 @@
     slim_token = pltpu.VMEM((shards, slim, tokens), BF)
     slim_frame = pltpu.VMEM((frames, *packed_shape(slots, slim)), BF)
     slim_row = pltpu.VMEM((shards, slim, CAP), BF)
+    operands = (
+        queries[0],
+        key_vectors[0],
+        value_vectors[0],
+        stream[0],
+        modulation[0],
+        output_bias,
+        router_weight.T,
+        expand_bias,
+        reduce_bias,
+        counts.T,
+        picked_rows,
+        output_weight.reshape(shards, cols, width),
+        expand_weight[0],
+        reduce_weight[0],
+    )
     layer_out = pl.pallas_call(
         layer_kernel,
         out_shape=jax.ShapeDtypeStruct((tokens, width), BF),
-        in_specs=[vmem] * 11 + [hbm] * 3,
+        in_specs=[hbm] * 14,
         out_specs=vmem,
         scratch_shapes=[
-            pltpu.VMEM((shards, cols, width), BF),
-            pltpu.VMEM((width, hidden), BF),
-            pltpu.VMEM((hidden, width), BF),
+            *[pltpu.VMEM(x.shape, x.dtype) for x in operands],
             pltpu.VMEM((3, shards, heads, HD, tokens), BF),
             pltpu.VMEM((3, shards, heads, HD, tokens), BF),
             pltpu.VMEM((shards, heads, HD, tokens), BF),
@@ -525,33 +562,21 @@
             pltpu.VMEM((frames, 8, 128), jnp.int32),
             [by_token] * 2 + [by_frame] * 2 + [by_row] * 3 + [by_frame] * 2 + [by_token] * 2,
             [slim_token] * 2 + [slim_frame] * 2 + [slim_row] * 3 + [slim_frame] * 2 + [slim_token] * 2,
-            pltpu.SemaphoreType.DMA((3,)),
-            pltpu.SemaphoreType.DMA((4 * heads, shards)),
-            pltpu.SemaphoreType.DMA((4 * heads, shards)),
-            pltpu.SemaphoreType.DMA((1 + 4 * steps, shards)),
-            pltpu.SemaphoreType.DMA((1 + 4 * steps, shards)),
-            pltpu.SemaphoreType.DMA((1 + 2 * steps, frames)),
-            pltpu.SemaphoreType.DMA((1 + 2 * steps, frames)),
+            pltpu.SemaphoreType.DMA((len(operands),)),
+            pltpu.SemaphoreType.DMA((1,)),
+            pltpu.SemaphoreType.DMA((heads,)),
+            pltpu.SemaphoreType.DMA((heads,)),
+            pltpu.SemaphoreType.DMA((1,)),
+            pltpu.SemaphoreType.DMA((shards,)),
+            pltpu.SemaphoreType.DMA((1 + 4 * steps,)),
+            pltpu.SemaphoreType.DMA((1 + 4 * steps,)),
+            pltpu.SemaphoreType.DMA((1 + 2 * steps,)),
+            pltpu.SemaphoreType.DMA((1 + 2 * steps,)),
         ],
         compiler_params=pltpu.CompilerParams(
             collective_id=1, has_side_effects=True, vmem_limit_bytes=60 << 20
         ),
-    )(
-        queries[0],
-        key_vectors[0],
-        value_vectors[0],
-        stream[0],
-        modulation[0],
-        output_bias,
-        router_weight.T,
-        expand_bias,
-        reduce_bias,
-        counts.T,
-        picked_rows,
-        output_weight.reshape(shards, cols, width),
-        expand_weight[0],
-        reduce_weight[0],
-    )
+    )(*operands)
     return layer_out[None]
 
 

time: 87.4 us -> 82.1 us (0.939)
  Pallas kernels: 85.3 us -> 80.1 us
    pallas_call x1, Pallas kernels: 85.3 us -> 80.1 us  [per_device(): pl.pallas_call(layer_kernel, out_shape=jax.ShapeDtypeStruct((tokens, widt...]
where the time goes in v2:
time: 82.1 us; the launch traced here: 82 us
  Pallas kernels  80.1 us (98%)
  local copies, waits for them, and re-layouts  1.92 us (2%)
    pallas_call x1, Pallas kernels, per_device(): pl.pallas_call(layer_kernel, out_shape=jax.ShapeDtypeStruct((tokens, widt...  80.1 us
    unnamed x1, local copies, waits for them, and re-layouts  1.92 us

profile of v2, /device:TPU:0, one launch (start us, length us, event | category | flops | bytes accessed | tf_op | source)
XLA Modules:
  0.0 82.0 jit_solution(17598664535640461248)
XLA Ops:
  0.0 80.1 %shard_map.136 = bf16[256,1152]{1,0:T(8,128)(2,1)} custom-call(bf16[256,1152]{1,0:T(8,128)(2,1)} %bitcast.15, bf16[256,1152]{1,0:T(8,128)(2,1)} %bitcast.16, bf16[256,1152]{1,0:T(8,128)(2,1)} %bitcast.17, bf16[256,1152]{1,0:T(8,128)(2,1)} %bitcast.18, f32[4,1152]{1,0:T(4,128)} %bitcast.19, f32[1152]{0:T(1024)} %refs_5_.1, bf16[8,1152]{1,0:T(8,128)(2,1)} %bitcast.20, ...), custom_call_target="tpu_custom_call" | custom-call | tf_op jit(solution)/shard_map/pallas_call | solution.py:542
  80.1 1.9 %copy.16 = bf16[1,256,1152]{2,1,0:T(8,128)(2,1)} copy(bf16[1,256,1152]{2,1,0:T(8,128)(2,1)} %bitcast.14) | data formatting | bytes 1179648
